TPU v7x, 32 devices: a whole 2x2x4 slice. The times are simulated.
32 devices in a mesh: ctx: 8 (over y, x, core), head: 4 (over z).
Axes of the slice: x: 2, y: 2, z: 4, core: 2. Of those that a mesh axis runs over, the one named last changes fastest.
Arguments:
- q_nope: bfloat16 [512, 8192], P('ctx', 'head'), may hold values from -0.59765625 to 0.59765625
- q_rope: bfloat16 [512, 4096], P('ctx', 'head'), may hold values from -6 to 6
- w_uk: bfloat16 [64, 128, 512], P('head'), may hold values from -0.5 to 0.5
- w_uv: bfloat16 [64, 512, 128], P('head'), may hold values from -0.25 to 0.25
- w_o: bfloat16 [8192, 7168], P('head'), may hold values from -0.0625 to 0.0625
- latent_cache: bfloat16 [576, 8192], P(None, 'ctx'), may hold values from -36 to 36
- group_start: int32 [1], replicated, may hold values from 2048 to 7680
Outputs:
- attention_out: bfloat16 [512, 7168], P('ctx', 'head')
All inputs are finite; a program needn't handle non-finite values.
Results may differ from a plain program's by a relative error of at most 0.02.
Values may be sent and summed in bfloat16 or wider, within the bound.
A program may use at most 128 MiB of HBM per device.

v0:
```python
import math
import jax
import jax.numpy as jnp
from jax import lax
from jax.sharding import PartitionSpec as P

LATENT = 512
ROPE = 64
NOPE = 128
VDIM = 128
masked_score = -1e30


def score_scale():
    return (NOPE + ROPE) ** (-0.5) * (0.1 * math.log(32.0) + 1.0) ** 2


def absorb_queries(q_nope, q_rope, w_uk):
    local_heads = w_uk.shape[0]
    tokens_here = q_nope.shape[0]
    nope_part = q_nope.reshape(tokens_here, local_heads, NOPE)
    latent_query = jnp.einsum(
        "thn,hnl->thl", nope_part, w_uk, preferred_element_type=jnp.float32
    ).astype(jnp.bfloat16)
    rope_part = q_rope.reshape(tokens_here, local_heads, ROPE)
    return jnp.concatenate([latent_query, rope_part], axis=2)


def block_scores_of(query_rows, row_position, key_block, key_start):
    scores = jnp.dot(query_rows, key_block, preferred_element_type=jnp.float32) * score_scale()
    key_position = key_start + jnp.arange(key_block.shape[1], dtype=jnp.int32)
    visible = key_position[None, :] <= row_position[:, None]
    return (jnp.where(visible, scores, masked_score), visible)


def latent_product(weights, key_block):
    return lax.dot_general(
        weights.astype(jnp.bfloat16),
        key_block[:LATENT],
        (((1,), (1,)), ((), ())),
        preferred_element_type=jnp.float32,
    )


def online_update(running, query_rows, row_position, key_block, key_start):
    best_sofar, denominator, numerator = running
    scores, visible = block_scores_of(query_rows, row_position, key_block, key_start)
    new_best = jnp.maximum(best_sofar, jnp.max(scores, axis=1))
    decay_factor = jnp.exp(best_sofar - new_best)
    weights = jnp.where(visible, jnp.exp(scores - new_best[:, None]), 0.0)
    denominator = denominator * decay_factor + jnp.sum(weights, axis=1)
    numerator = numerator * decay_factor[:, None] + latent_product(weights, key_block)
    return (new_best, denominator, numerator)


def value_heads(latent_out, w_uv):
    leading = latent_out.astype(jnp.bfloat16)
    remainder = (latent_out - leading.astype(jnp.float32)).astype(jnp.bfloat16)
    first_term = jnp.einsum("thl,hlv->thv", leading, w_uv, preferred_element_type=jnp.float32)
    second_term = jnp.einsum("thl,hlv->thv", remainder, w_uv, preferred_element_type=jnp.float32)
    return first_term + second_term


def on_device(q_nope, q_rope, w_uk, w_uv, w_o, latent_cache, group_start):
    local_heads = w_uk.shape[0]
    tokens_here = q_nope.shape[0]
    queries = absorb_queries(q_nope, q_rope, w_uk)
    query_width = queries.shape[2]
    query_rows = queries.reshape(tokens_here * local_heads, query_width)
    first_token = group_start[0] + lax.axis_index("ctx") * tokens_here
    token_position = first_token + jnp.arange(tokens_here, dtype=jnp.int32)
    row_position = jnp.repeat(token_position, local_heads)
    last_position = first_token + tokens_here - 1
    row_total = query_rows.shape[0]
    initial = (
        jnp.full((row_total,), masked_score, jnp.float32),
        jnp.zeros((row_total,), jnp.float32),
        jnp.zeros((row_total, LATENT), jnp.float32),
    )
    cache_piece = lax.all_gather(latent_cache, "ctx", axis=1, tiled=True)
    span_keys = cache_piece.shape[1]
    step_keys = math.gcd(span_keys, 1024)

    def advance(position, current):
        key_block = lax.dynamic_slice_in_dim(cache_piece, position * step_keys, step_keys, 1)
        key_start = position * step_keys
        return lax.cond(
            key_start <= last_position,
            lambda held_state: online_update(
                held_state, query_rows, row_position, key_block, key_start
            ),
            lambda held_state: held_state,
            current,
        )

    best_all, denominator, numerator = lax.fori_loop(0, span_keys // step_keys, advance, initial)
    latent_out = (numerator / denominator[:, None]).reshape(tokens_here, local_heads, LATENT)
    head_values = value_heads(latent_out, w_uv)
    head_out = head_values.reshape(tokens_here, local_heads * VDIM).astype(jnp.bfloat16)
    mixed_columns = lax.psum_scatter(
        lax.dot_general(
            w_o, head_out, (((0,), (1,)), ((), ())), preferred_element_type=jnp.float32
        ).astype(jnp.bfloat16),
        "head",
        scatter_dimension=0,
        tiled=True,
    ).astype(jnp.float32)
    return mixed_columns.T.astype(jnp.bfloat16)


def solution(mesh):
    placed = (
        P("ctx", "head"),
        P("ctx", "head"),
        P("head", None, None),
        P("head", None, None),
        P("head", None),
        P(None, "ctx"),
        P(),
    )
    return jax.shard_map(
        on_device, mesh=mesh, in_specs=placed, out_specs=P("ctx", "head"), check_vma=False
    )
```

profile of v0, /device:TPU:0, one launch (start us, length us, event | category | flops | bytes accessed | tf_op | source)
XLA Modules:
  0.0 189.2 jit_solution(10341991162294786922)
XLA Ops:
  12.3 58.4 %all-gather.2.cloned.1.call-done = bf16[576,8192]{1,0:T(8,128)(2,1)} async-done(((bf16[576,1024]{1,0:T(8,128)(2,1)}), bf16[576,8192]{1,0:T(8,128)(2,1)}) %all-gather.2.cloned.1.call-update) | async-done | bytes 9437200 | tf_op jit(solution)/shard_map/all_gather | solution.py:80
  70.7 1.6 broadcast_in_dim.29
  72.3 57.2 %while.18 = (s32[]{:T(128)}, f32[1024]{0:T(1024)S(1)}, f32[1024]{0:T(1024)S(1)}, f32[1024,512]{1,0:T(8,128)}, s32[]{:T(128)}, /*index=5*/bf16[576,8192]{1,0:T(8,...) while((s32[]{:T(128)}, f32[1024]{0:T(1024)S(1)}, ...), condition=%wide.region_5.6_spmd.clone, body=%wide.region_0.5_spmd.clone.sunk | while | flops 2299530240 | bytes 37069400 | solution.py:96
  72.3 9.5 %conditional.3 = ((f32[1024]{0:T(1024)S(1)}, f32[1024]{0:T(1024)S(1)}, f32[1024,512]{1,0:T(8,128)})) conditional(s32[]{:T(128)} %convert_element_type.82, (f32[1024]{0:T(1024)S(1)}, f32[1024]{0:T(1024)S(1)}, f32[1024,512]{1,0:T(8,128)}) %tuple.50, (s32[]{:T(128)}, s32[64]{0:T(128)S(1)}, bf16[576,8192]{1,0:T(8,128)(2,1)}, ...), branch_computations={%region_1.0_spmd, %region_2.4_spmd} | conditional | flops 2299530240 | bytes 37069192 | solution.py:87
  72.4 3.4 %fusion.2 = (f32[1024]{0:T(1024)S(1)}, f32[1024,1024]{1,0:T(8,128)S(1)}) fusion(s32[1024]{0:T(1024)S(1)} %le.27, s32[1024]{0:T(1024)S(1)} %iota_add_fusion, bf16[1024,576]{1,0:T(8,128)(2,1)S(1)} %get-tuple-element.214, bf16[576,8192]{1,0:T(8,128)(2,1)} %get-tuple-element.213, s32[]{:T(128)S(6)} %select_n.18), kind=kOutput, calls=%fused_computation.3 | convolution fusion | flops 1212152832 | bytes 6565892 | tf_op jit(solution)/shard_map/while/body/eval_jaxpr/cond/branch_1_fun/dot_general | solution.py:30
  77.5 3.0 %multiply_add_fusion = f32[1024,512]{1,0:T(8,128)S(1)} fusion(f32[1024,512]{1,0:T(8,128)S(1)} %copy-done.1, f32[1024,1024]{1,0:T(8,128)S(1)} %get-tuple-element.275, f32[1024]{0:T(1024)S(1)} %max.4, s32[1024]{0:T(1024)S(1)} %le.27, s32[1024]{0:T(1024)S(1)} %iota_add_fusion, bf16[576,8192]{1,0:T(8,128)(2,1)} %get-tuple-element.213, s32[]{:T(128)S(6)} %select_n.18, ...), kind=kOutput, calls=%fused_computation.6 | convolution fusion | flops 1081081856 | bytes 9453572 | tf_op jit(solution)/shard_map/while/body/eval_jaxpr/cond/branch_1_fun/dot_general | solution.py:37
  81.8 9.5 %conditional.3 = ((f32[1024]{0:T(1024)S(1)}, f32[1024]{0:T(1024)S(1)}, f32[1024,512]{1,0:T(8,128)})) conditional(s32[]{:T(128)} %convert_element_type.82, (f32[1024]{0:T(1024)S(1)}, f32[1024]{0:T(1024)S(1)}, f32[1024,512]{1,0:T(8,128)}) %tuple.50, (s32[]{:T(128)}, s32[64]{0:T(128)S(1)}, bf16[576,8192]{1,0:T(8,128)(2,1)}, ...), branch_computations={%region_1.0_spmd, %region_2.4_spmd} | conditional | flops 2299530240 | bytes 37069192 | solution.py:87
  82.0 3.4 %fusion.2 = (f32[1024]{0:T(1024)S(1)}, f32[1024,1024]{1,0:T(8,128)S(1)}) fusion(s32[1024]{0:T(1024)S(1)} %le.27, s32[1024]{0:T(1024)S(1)} %iota_add_fusion, bf16[1024,576]{1,0:T(8,128)(2,1)S(1)} %get-tuple-element.214, bf16[576,8192]{1,0:T(8,128)(2,1)} %get-tuple-element.213, s32[]{:T(128)S(6)} %select_n.18), kind=kOutput, calls=%fused_computation.3 | convolution fusion | flops 1212152832 | bytes 6565892 | tf_op jit(solution)/shard_map/while/body/eval_jaxpr/cond/branch_1_fun/dot_general | solution.py:30
  87.0 3.0 %multiply_add_fusion = f32[1024,512]{1,0:T(8,128)S(1)} fusion(f32[1024,512]{1,0:T(8,128)S(1)} %copy-done.1, f32[1024,1024]{1,0:T(8,128)S(1)} %get-tuple-element.275, f32[1024]{0:T(1024)S(1)} %max.4, s32[1024]{0:T(1024)S(1)} %le.27, s32[1024]{0:T(1024)S(1)} %iota_add_fusion, bf16[576,8192]{1,0:T(8,128)(2,1)} %get-tuple-element.213, s32[]{:T(128)S(6)} %select_n.18, ...), kind=kOutput, calls=%fused_computation.6 | convolution fusion | flops 1081081856 | bytes 9453572 | tf_op jit(solution)/shard_map/while/body/eval_jaxpr/cond/branch_1_fun/dot_general | solution.py:37
  91.3 9.5 %conditional.3 = ((f32[1024]{0:T(1024)S(1)}, f32[1024]{0:T(1024)S(1)}, f32[1024,512]{1,0:T(8,128)})) conditional(s32[]{:T(128)} %convert_element_type.82, (f32[1024]{0:T(1024)S(1)}, f32[1024]{0:T(1024)S(1)}, f32[1024,512]{1,0:T(8,128)}) %tuple.50, (s32[]{:T(128)}, s32[64]{0:T(128)S(1)}, bf16[576,8192]{1,0:T(8,128)(2,1)}, ...), branch_computations={%region_1.0_spmd, %region_2.4_spmd} | conditional | flops 2299530240 | bytes 37069192 | solution.py:87
  91.5 3.4 %fusion.2 = (f32[1024]{0:T(1024)S(1)}, f32[1024,1024]{1,0:T(8,128)S(1)}) fusion(s32[1024]{0:T(1024)S(1)} %le.27, s32[1024]{0:T(1024)S(1)} %iota_add_fusion, bf16[1024,576]{1,0:T(8,128)(2,1)S(1)} %get-tuple-element.214, bf16[576,8192]{1,0:T(8,128)(2,1)} %get-tuple-element.213, s32[]{:T(128)S(6)} %select_n.18), kind=kOutput, calls=%fused_computation.3 | convolution fusion | flops 1212152832 | bytes 6565892 | tf_op jit(solution)/shard_map/while/body/eval_jaxpr/cond/branch_1_fun/dot_general | solution.py:30
  96.6 3.0 %multiply_add_fusion = f32[1024,512]{1,0:T(8,128)S(1)} fusion(f32[1024,512]{1,0:T(8,128)S(1)} %copy-done.1, f32[1024,1024]{1,0:T(8,128)S(1)} %get-tuple-element.275, f32[1024]{0:T(1024)S(1)} %max.4, s32[1024]{0:T(1024)S(1)} %le.27, s32[1024]{0:T(1024)S(1)} %iota_add_fusion, bf16[576,8192]{1,0:T(8,128)(2,1)} %get-tuple-element.213, s32[]{:T(128)S(6)} %select_n.18, ...), kind=kOutput, calls=%fused_computation.6 | convolution fusion | flops 1081081856 | bytes 9453572 | tf_op jit(solution)/shard_map/while/body/eval_jaxpr/cond/branch_1_fun/dot_general | solution.py:37
  100.9 9.5 %conditional.3 = ((f32[1024]{0:T(1024)S(1)}, f32[1024]{0:T(1024)S(1)}, f32[1024,512]{1,0:T(8,128)})) conditional(s32[]{:T(128)} %convert_element_type.82, (f32[1024]{0:T(1024)S(1)}, f32[1024]{0:T(1024)S(1)}, f32[1024,512]{1,0:T(8,128)}) %tuple.50, (s32[]{:T(128)}, s32[64]{0:T(128)S(1)}, bf16[576,8192]{1,0:T(8,128)(2,1)}, ...), branch_computations={%region_1.0_spmd, %region_2.4_spmd} | conditional | flops 2299530240 | bytes 37069192 | solution.py:87
  101.0 3.4 %fusion.2 = (f32[1024]{0:T(1024)S(1)}, f32[1024,1024]{1,0:T(8,128)S(1)}) fusion(s32[1024]{0:T(1024)S(1)} %le.27, s32[1024]{0:T(1024)S(1)} %iota_add_fusion, bf16[1024,576]{1,0:T(8,128)(2,1)S(1)} %get-tuple-element.214, bf16[576,8192]{1,0:T(8,128)(2,1)} %get-tuple-element.213, s32[]{:T(128)S(6)} %select_n.18), kind=kOutput, calls=%fused_computation.3 | convolution fusion | flops 1212152832 | bytes 6565892 | tf_op jit(solution)/shard_map/while/body/eval_jaxpr/cond/branch_1_fun/dot_general | solution.py:30
  106.1 3.0 %multiply_add_fusion = f32[1024,512]{1,0:T(8,128)S(1)} fusion(f32[1024,512]{1,0:T(8,128)S(1)} %copy-done.1, f32[1024,1024]{1,0:T(8,128)S(1)} %get-tuple-element.275, f32[1024]{0:T(1024)S(1)} %max.4, s32[1024]{0:T(1024)S(1)} %le.27, s32[1024]{0:T(1024)S(1)} %iota_add_fusion, bf16[576,8192]{1,0:T(8,128)(2,1)} %get-tuple-element.213, s32[]{:T(128)S(6)} %select_n.18, ...), kind=kOutput, calls=%fused_computation.6 | convolution fusion | flops 1081081856 | bytes 9453572 | tf_op jit(solution)/shard_map/while/body/eval_jaxpr/cond/branch_1_fun/dot_general | solution.py:37
  110.4 9.5 %conditional.3 = ((f32[1024]{0:T(1024)S(1)}, f32[1024]{0:T(1024)S(1)}, f32[1024,512]{1,0:T(8,128)})) conditional(s32[]{:T(128)} %convert_element_type.82, (f32[1024]{0:T(1024)S(1)}, f32[1024]{0:T(1024)S(1)}, f32[1024,512]{1,0:T(8,128)}) %tuple.50, (s32[]{:T(128)}, s32[64]{0:T(128)S(1)}, bf16[576,8192]{1,0:T(8,128)(2,1)}, ...), branch_computations={%region_1.0_spmd, %region_2.4_spmd} | conditional | flops 2299530240 | bytes 37069192 | solution.py:87
  110.6 3.4 %fusion.2 = (f32[1024]{0:T(1024)S(1)}, f32[1024,1024]{1,0:T(8,128)S(1)}) fusion(s32[1024]{0:T(1024)S(1)} %le.27, s32[1024]{0:T(1024)S(1)} %iota_add_fusion, bf16[1024,576]{1,0:T(8,128)(2,1)S(1)} %get-tuple-element.214, bf16[576,8192]{1,0:T(8,128)(2,1)} %get-tuple-element.213, s32[]{:T(128)S(6)} %select_n.18), kind=kOutput, calls=%fused_computation.3 | convolution fusion | flops 1212152832 | bytes 6565892 | tf_op jit(solution)/shard_map/while/body/eval_jaxpr/cond/branch_1_fun/dot_general | solution.py:30
  115.6 3.0 %multiply_add_fusion = f32[1024,512]{1,0:T(8,128)S(1)} fusion(f32[1024,512]{1,0:T(8,128)S(1)} %copy-done.1, f32[1024,1024]{1,0:T(8,128)S(1)} %get-tuple-element.275, f32[1024]{0:T(1024)S(1)} %max.4, s32[1024]{0:T(1024)S(1)} %le.27, s32[1024]{0:T(1024)S(1)} %iota_add_fusion, bf16[576,8192]{1,0:T(8,128)(2,1)} %get-tuple-element.213, s32[]{:T(128)S(6)} %select_n.18, ...), kind=kOutput, calls=%fused_computation.6 | convolution fusion | flops 1081081856 | bytes 9453572 | tf_op jit(solution)/shard_map/while/body/eval_jaxpr/cond/branch_1_fun/dot_general | solution.py:37
  120.0 9.5 %conditional.3 = ((f32[1024]{0:T(1024)S(1)}, f32[1024]{0:T(1024)S(1)}, f32[1024,512]{1,0:T(8,128)})) conditional(s32[]{:T(128)} %convert_element_type.82, (f32[1024]{0:T(1024)S(1)}, f32[1024]{0:T(1024)S(1)}, f32[1024,512]{1,0:T(8,128)}) %tuple.50, (s32[]{:T(128)}, s32[64]{0:T(128)S(1)}, bf16[576,8192]{1,0:T(8,128)(2,1)}, ...), branch_computations={%region_1.0_spmd, %region_2.4_spmd} | conditional | flops 2299530240 | bytes 37069192 | solution.py:87
  120.1 3.4 %fusion.2 = (f32[1024]{0:T(1024)S(1)}, f32[1024,1024]{1,0:T(8,128)S(1)}) fusion(s32[1024]{0:T(1024)S(1)} %le.27, s32[1024]{0:T(1024)S(1)} %iota_add_fusion, bf16[1024,576]{1,0:T(8,128)(2,1)S(1)} %get-tuple-element.214, bf16[576,8192]{1,0:T(8,128)(2,1)} %get-tuple-element.213, s32[]{:T(128)S(6)} %select_n.18), kind=kOutput, calls=%fused_computation.3 | convolution fusion | flops 1212152832 | bytes 6565892 | tf_op jit(solution)/shard_map/while/body/eval_jaxpr/cond/branch_1_fun/dot_general | solution.py:30
  125.2 3.0 %multiply_add_fusion = f32[1024,512]{1,0:T(8,128)S(1)} fusion(f32[1024,512]{1,0:T(8,128)S(1)} %copy-done.1, f32[1024,1024]{1,0:T(8,128)S(1)} %get-tuple-element.275, f32[1024]{0:T(1024)S(1)} %max.4, s32[1024]{0:T(1024)S(1)} %le.27, s32[1024]{0:T(1024)S(1)} %iota_add_fusion, bf16[576,8192]{1,0:T(8,128)(2,1)} %get-tuple-element.213, s32[]{:T(128)S(6)} %select_n.18, ...), kind=kOutput, calls=%fused_computation.6 | convolution fusion | flops 1081081856 | bytes 9453572 | tf_op jit(solution)/shard_map/while/body/eval_jaxpr/cond/branch_1_fun/dot_general | solution.py:37
  129.5 1.9 %broadcast_divide_fusion = f32[1024,512]{1,0:T(8,128)S(1)} fusion(f32[1024,512]{1,0:T(8,128)} %get-tuple-element.231, f32[1024]{0:T(1024)S(1)} %get-tuple-element.232), kind=kLoop, calls=%fused_computation.31 | loop fusion | flops 524288 | bytes 4198400 | tf_op jit(solution)/shard_map/div | solution.py:97
  134.4 13.1 %fusion.18 = bf16[7168,64]{0,1:T(8,128)(2,1)} fusion(bf16[2048,7168]{1,0:T(8,128)(2,1)} %param.15, bf16[16,8,8,128]{3,2,1,0:T(8,128)(2,1)S(1)} %fusion.22), kind=kOutput, calls=%fused_computation.21 | convolution fusion | flops 1879506944 | bytes 30539776 | tf_op jit(solution)/shard_map/dot_general | solution.py:101
  147.5 34.9 %reduce-scatter.2.cloned.1.call-done = bf16[1792,64]{0,1:T(8,128)(2,1)} async-done(((bf16[7168,64]{0,1:T(8,128)(2,1)}), bf16[1792,64]{0,1:T(8,128)(2,1)}) %reduce-scatter.2.cloned.1.call-update) | async-done | bytes 229392 | tf_op jit(solution)/shard_map/reduce_scatter | solution.py:100
  (87 shorter events, 26.2 us)
Async XLA Ops:
  6.5 2.5 %copy-start = (bf16[16,128,512]{2,1,0:T(8,128)(2,1)S(1)}, bf16[16,128,512]{2,1,0:T(8,128)(2,1)}, u32[]{:S(2)}) copy-start(bf16[16,128,512]{2,1,0:T(8,128)(2,1)} %param.13) | copy-start | bytes 6291460
  6.5 64.2 %all-gather.2.cloned.1.call-start = ((), (), s32[]{:S(2)}) async-start(), calls=%async_computation.1 | async-start | bytes 10616832 | tf_op jit(solution)/shard_map/all_gather | solution.py:80
  7.3 175.1 %reduce-scatter.2.cloned.1.call-start = ((), (), s32[]{:S(2)}) async-start(), calls=%async_computation.2 | async-start | bytes 1146880 | tf_op jit(solution)/shard_map/reduce_scatter | solution.py:100
  12.3 60.0 %copy-start.4 = (bf16[1024,576]{1,0:T(8,128)(2,1)S(1)}, bf16[1024,576]{1,0:T(8,128)(2,1)}, u32[]{:S(2)}) copy-start(bf16[1024,576]{1,0:T(8,128)(2,1)} %pad_maximum_fusion) | copy-start | bytes 3538948
  75.9 1.6 copy-start.1
  80.5 1.3 copy-start.2
  85.4 1.6 copy-start.1
  90.0 1.3 copy-start.2
  95.0 1.6 copy-start.1
  99.6 1.3 copy-start.2
  104.5 1.6 copy-start.1
  109.1 1.3 copy-start.2
  114.0 1.6 copy-start.1
  118.6 1.3 copy-start.2
  123.6 1.6 copy-start.1
  128.2 1.3 copy-start.2
  129.5 2.2 %copy-start.3 = (bf16[16,512,128]{2,1,0:T(8,128)(2,1)S(1)}, bf16[16,512,128]{2,1,0:T(8,128)(2,1)}, u32[]{:S(2)}) copy-start(bf16[16,512,128]{2,1,0:T(8,128)(2,1)} %param.14) | copy-start | bytes 6291460
Sparse Core Ops, SparseCore 0:
  9.2 61.4 all-gather.1
  147.6 34.7 reduce-scatter.1
where the time goes:
time: 190 us; the launch traced here: 189 us
  waiting for transfers between devices  94 us (49%)
  matrix products  55.8 us (29%)
  between operations  14.1 us (7%)
  other arithmetic  12.5 us (7%)
  local copies, waits for them, and re-layouts  12.4 us (7%)
    all_gather x1, waiting for transfers between devices, on_device(): cache_piece = lax.all_gather(latent_cache, 'ctx', axis=1, tiled=True)  58.4 us
    reduce_scatter x1, waiting for transfers between devices, on_device(): lax.psum_scatter(lax.dot_general(w_o, head_out, (((0,), (1,)), ((), ())),...  34.9 us
    dot_general x6, matrix products, block_scores_of(): jnp.dot(query_rows, key_block, preferred_element_type=jnp.float32)  20.6 us
    dot_general x6, matrix products, latent_product(): lax.dot_general(weights.astype(jnp.bfloat16), key_block[:LATENT], (((1,),...  18.1 us
    dot_general x1, matrix products, on_device(): lax.dot_general(w_o, head_out, (((0,), (1,)), ((), ())), preferred_elemen...  13.1 us
    reduce_sum x6, other arithmetic, online_update(): denominator = denominator * decay_factor + jnp.sum(weights, axis=1)  9.27 us
    cond x30, local copies, waits for them, and re-layouts  7.95 us
  transfers between devices with their start and end apart: 2, of which 2 were waited for; matrix products, arithmetic and copies ran while one was open for 2% of the time, Pallas kernels for 0%

commit v1 on v0

--- a/solution.py
+++ b/solution.py
@@ -77,7 +77,13 @@
         jnp.zeros((row_total,), jnp.float32),
         jnp.zeros((row_total, LATENT), jnp.float32),
     )
-    cache_piece = lax.all_gather(latent_cache, "ctx", axis=1, tiled=True)
+    count = lax.axis_size("ctx")
+    moving, blocks = (latent_cache, [latent_cache])
+    for _ in range(count - 1):
+        moving = lax.ppermute(moving, "ctx", [(i, (i + 1) % count) for i in range(count)])
+        blocks.insert(0, moving)
+    flat = jnp.concatenate(blocks, axis=1)
+    cache_piece = jnp.roll(flat, (lax.axis_index("ctx") + 1) * latent_cache.shape[1], axis=1)
     span_keys = cache_piece.shape[1]
     step_keys = math.gcd(span_keys, 1024)
 

time: 190 us -> 269 us (1.42)
  waiting for transfers between devices: 94 us -> 143 us
  local copies, waits for them, and re-layouts: 12.4 us -> 39.8 us
    ppermute x0 -> x7, waiting for transfers between devices: none -> 110 us  [on_device(): lax.ppermute(moving, 'ctx', [(i, (i + 1) % count) for i in range(count)])]
    all_gather x1 -> x0, waiting for transfers between devices: 58.4 us -> none  [on_device(): cache_piece = lax.all_gather(latent_cache, 'ctx', axis=1, tiled=True)]
    unnamed x6 -> x47, local copies, waits for them, and re-layouts: 0.27 us -> 27.2 us
    dynamic_slice x0 -> x1, local copies, waits for them, and re-layouts: none -> 8.62 us  [on_device(): jnp.roll(flat, (lax.axis_index('ctx') + 1) * latent_cache.shape[1], axis=1)]
    cond x30 -> x6, local copies, waits for them, and re-layouts: 7.95 us -> 0.02 us
  transfers between devices with their start and end apart: 2 -> 8, of which waited for: 2 -> 8; matrix products, arithmetic and copies ran while one was open for 2% -> 2% of each run, Pallas kernels for 0% -> 0%
where the time goes in v1:
time: 269 us; the launch traced here: 268 us
  waiting for transfers between devices  143 us (53%)
  matrix products  56.1 us (21%)
  local copies, waits for them, and re-layouts  39.8 us (15%)
  between operations  14.2 us (5%)
  other arithmetic  13.8 us (5%)
    ppermute x7, waiting for transfers between devices, on_device(): lax.ppermute(moving, 'ctx', [(i, (i + 1) % count) for i in range(count)])  110 us
    reduce_scatter x1, waiting for transfers between devices, on_device(): lax.psum_scatter(lax.dot_general(w_o, head_out, (((0,), (1,)), ((), ())),...  32.5 us
    unnamed x47, local copies, waits for them, and re-layouts  27.2 us
    dot_general x6, matrix products, block_scores_of(): jnp.dot(query_rows, key_block, preferred_element_type=jnp.float32)  20.5 us
    dot_general x6, matrix products, latent_product(): lax.dot_general(weights.astype(jnp.bfloat16), key_block[:LATENT], (((1,),...  18.1 us
    dot_general x1, matrix products, on_device(): lax.dot_general(w_o, head_out, (((0,), (1,)), ((), ())), preferred_elemen...  13.2 us
    reduce_sum x6, other arithmetic, online_update(): denominator = denominator * decay_factor + jnp.sum(weights, axis=1)  9.26 us
    dynamic_slice x1, local copies, waits for them, and re-layouts, on_device(): jnp.roll(flat, (lax.axis_index('ctx') + 1) * latent_cache.shape[1], axis=1)  8.62 us
  transfers between devices with their start and end apart: 8, of which 8 were waited for; matrix products, arithmetic and copies ran while one was open for 2% of the time, Pallas kernels for 0%

profile of v1, /device:TPU:0, one launch (start us, length us, event | category | flops | bytes accessed | tf_op | source)
XLA Modules:
  0.0 267.9 jit_solution(10075522630338084650)
XLA Ops:
  7.0 17.0 %collective-permute-done = bf16[576,1024]{1,0:T(8,128)(2,1)S(1)} collective-permute-done((bf16[576,1024]{1,0:T(8,128)(2,1)}, bf16[576,1024]{1,0:T(8,128)(2,1)S(1)}, u32[]{:S(2)}, u32[]{:S(2)}) %collective-permute-start) | collective-permute-done | bytes 1179680 | tf_op jit(solution)/shard_map/ppermute | solution.py:83
  24.0 16.5 %collective-permute-done.1 = bf16[576,1024]{1,0:T(8,128)(2,1)S(1)} collective-permute-done((bf16[576,1024]{1,0:T(8,128)(2,1)S(1)}, bf16[576,1024]{1,0:T(8,128)(2,1)S(1)}, u32[]{:S(2)}, u32[]{:S(2)}) %collective-permute-start.1) | collective-permute-done | bytes 1179680 | tf_op jit(solution)/shard_map/ppermute | solution.py:83
  41.6 16.5 %collective-permute-done.2 = bf16[576,1024]{1,0:T(8,128)(2,1)S(1)} collective-permute-done((bf16[576,1024]{1,0:T(8,128)(2,1)S(1)}, bf16[576,1024]{1,0:T(8,128)(2,1)S(1)}, u32[]{:S(2)}, u32[]{:S(2)}) %collective-permute-start.2) | collective-permute-done | bytes 1179680 | tf_op jit(solution)/shard_map/ppermute | solution.py:83
  59.1 16.5 %collective-permute-done.3 = bf16[576,1024]{1,0:T(8,128)(2,1)S(1)} collective-permute-done((bf16[576,1024]{1,0:T(8,128)(2,1)S(1)}, bf16[576,1024]{1,0:T(8,128)(2,1)S(1)}, u32[]{:S(2)}, u32[]{:S(2)}) %collective-permute-start.3) | collective-permute-done | bytes 1179680 | tf_op jit(solution)/shard_map/ppermute | solution.py:83
  76.8 16.5 %collective-permute-done.4 = bf16[576,1024]{1,0:T(8,128)(2,1)S(1)} collective-permute-done((bf16[576,1024]{1,0:T(8,128)(2,1)S(1)}, bf16[576,1024]{1,0:T(8,128)(2,1)S(1)}, u32[]{:S(2)}, u32[]{:S(2)}) %collective-permute-start.4) | collective-permute-done | bytes 1179680 | tf_op jit(solution)/shard_map/ppermute | solution.py:83
  94.3 16.6 %collective-permute-done.5 = bf16[576,1024]{1,0:T(8,128)(2,1)} collective-permute-done((bf16[576,1024]{1,0:T(8,128)(2,1)S(1)}, bf16[576,1024]{1,0:T(8,128)(2,1)}, u32[]{:S(2)}, u32[]{:S(2)}) %collective-permute-start.5) | collective-permute-done | bytes 1179680 | tf_op jit(solution)/shard_map/ppermute | solution.py:83
  117.3 10.5 %collective-permute-done.6 = bf16[576,1024]{1,0:T(8,128)(2,1)} collective-permute-done((bf16[576,1024]{1,0:T(8,128)(2,1)}, bf16[576,1024]{1,0:T(8,128)(2,1)}, u32[]{:S(2)}, u32[]{:S(2)}) %collective-permute-start.6) | collective-permute-done | bytes 1179680 | tf_op jit(solution)/shard_map/ppermute | solution.py:83
  150.6 8.6 %constant_dynamic-slice_fusion = bf16[576,8192]{1,0:T(8,128)(2,1)} fusion(bf16[576,16384]{1,0:T(8,128)(2,1)} %constant_dynamic-update-slice_fusion, s32[]{:T(128)S(6)} %select_n.35), kind=kLoop, calls=%fused_computation.53 | loop fusion | bytes 18874372 | tf_op jit(solution)/shard_map/jit(_roll_dynamic)/dynamic_slice | solution.py:86
  159.5 49.7 %while.18 = (s32[]{:T(128)}, f32[1024]{0:T(1024)S(1)}, f32[1024]{0:T(1024)S(1)}, f32[1024,512]{1,0:T(8,128)S(1)}, s32[]{:T(128)}, /*index=5*/bf16[576,8192]{1,0:...) while((s32[]{:T(128)}, f32[1024]{0:T(1024)S(1)}, ...), condition=%wide.region_5.6_spmd.clone, body=%wide.region_0.5_spmd.clone.sunk | while | flops 2299530240 | bytes 20292124 | solution.py:102
  159.7 8.2 %conditional.3 = ((f32[1024]{0:T(1024)S(1)}, f32[1024]{0:T(1024)S(1)}, f32[1024,512]{1,0:T(8,128)S(1)})) conditional(s32[]{:T(128)} %convert_element_type.82, (f32[1024]{0:T(1024)S(1)}, f32[1024]{0:T(1024)S(1)}, f32[1024,512]{1,0:T(8,128)S(1)}) %tuple.50, (s32[]{:T(128)}, s32[64]{0:T(128)S(1)}, bf16[576,8192]{1,0:T(8,128)(2,1)}, ...), branch_computations={%region_1.1_spmd, %region_2.4_spmd} | conditional | flops 2299530240 | bytes 20291918 | solution.py:93
  159.9 3.4 %fusion.2 = (f32[1024]{0:T(1024)S(1)}, f32[1024,1024]{1,0:T(8,128)S(1)}) fusion(s32[1024]{0:T(1024)S(1)} %le.27, s32[1024]{0:T(1024)S(1)} %iota_add_fusion, bf16[1024,576]{1,0:T(8,128)(2,1)S(1)} %get-tuple-element.214, bf16[576,8192]{1,0:T(8,128)(2,1)} %get-tuple-element.213, s32[]{:T(128)S(6)} %select_n.29), kind=kOutput, calls=%fused_computation.3 | convolution fusion | flops 1212152832 | bytes 6565892 | tf_op jit(solution)/shard_map/while/body/eval_jaxpr/cond/branch_1_fun/dot_general | solution.py:30
  167.9 8.2 %conditional.3 = ((f32[1024]{0:T(1024)S(1)}, f32[1024]{0:T(1024)S(1)}, f32[1024,512]{1,0:T(8,128)S(1)})) conditional(s32[]{:T(128)} %convert_element_type.82, (f32[1024]{0:T(1024)S(1)}, f32[1024]{0:T(1024)S(1)}, f32[1024,512]{1,0:T(8,128)S(1)}) %tuple.50, (s32[]{:T(128)}, s32[64]{0:T(128)S(1)}, bf16[576,8192]{1,0:T(8,128)(2,1)}, ...), branch_computations={%region_1.1_spmd, %region_2.4_spmd} | conditional | flops 2299530240 | bytes 20291918 | solution.py:93
  168.1 3.4 %fusion.2 = (f32[1024]{0:T(1024)S(1)}, f32[1024,1024]{1,0:T(8,128)S(1)}) fusion(s32[1024]{0:T(1024)S(1)} %le.27, s32[1024]{0:T(1024)S(1)} %iota_add_fusion, bf16[1024,576]{1,0:T(8,128)(2,1)S(1)} %get-tuple-element.214, bf16[576,8192]{1,0:T(8,128)(2,1)} %get-tuple-element.213, s32[]{:T(128)S(6)} %select_n.29), kind=kOutput, calls=%fused_computation.3 | convolution fusion | flops 1212152832 | bytes 6565892 | tf_op jit(solution)/shard_map/while/body/eval_jaxpr/cond/branch_1_fun/dot_general | solution.py:30
  176.2 8.2 %conditional.3 = ((f32[1024]{0:T(1024)S(1)}, f32[1024]{0:T(1024)S(1)}, f32[1024,512]{1,0:T(8,128)S(1)})) conditional(s32[]{:T(128)} %convert_element_type.82, (f32[1024]{0:T(1024)S(1)}, f32[1024]{0:T(1024)S(1)}, f32[1024,512]{1,0:T(8,128)S(1)}) %tuple.50, (s32[]{:T(128)}, s32[64]{0:T(128)S(1)}, bf16[576,8192]{1,0:T(8,128)(2,1)}, ...), branch_computations={%region_1.1_spmd, %region_2.4_spmd} | conditional | flops 2299530240 | bytes 20291918 | solution.py:93
  176.4 3.4 %fusion.2 = (f32[1024]{0:T(1024)S(1)}, f32[1024,1024]{1,0:T(8,128)S(1)}) fusion(s32[1024]{0:T(1024)S(1)} %le.27, s32[1024]{0:T(1024)S(1)} %iota_add_fusion, bf16[1024,576]{1,0:T(8,128)(2,1)S(1)} %get-tuple-element.214, bf16[576,8192]{1,0:T(8,128)(2,1)} %get-tuple-element.213, s32[]{:T(128)S(6)} %select_n.29), kind=kOutput, calls=%fused_computation.3 | convolution fusion | flops 1212152832 | bytes 6565892 | tf_op jit(solution)/shard_map/while/body/eval_jaxpr/cond/branch_1_fun/dot_general | solution.py:30
  184.4 8.2 %conditional.3 = ((f32[1024]{0:T(1024)S(1)}, f32[1024]{0:T(1024)S(1)}, f32[1024,512]{1,0:T(8,128)S(1)})) conditional(s32[]{:T(128)} %convert_element_type.82, (f32[1024]{0:T(1024)S(1)}, f32[1024]{0:T(1024)S(1)}, f32[1024,512]{1,0:T(8,128)S(1)}) %tuple.50, (s32[]{:T(128)}, s32[64]{0:T(128)S(1)}, bf16[576,8192]{1,0:T(8,128)(2,1)}, ...), branch_computations={%region_1.1_spmd, %region_2.4_spmd} | conditional | flops 2299530240 | bytes 20291918 | solution.py:93
  184.6 3.4 %fusion.2 = (f32[1024]{0:T(1024)S(1)}, f32[1024,1024]{1,0:T(8,128)S(1)}) fusion(s32[1024]{0:T(1024)S(1)} %le.27, s32[1024]{0:T(1024)S(1)} %iota_add_fusion, bf16[1024,576]{1,0:T(8,128)(2,1)S(1)} %get-tuple-element.214, bf16[576,8192]{1,0:T(8,128)(2,1)} %get-tuple-element.213, s32[]{:T(128)S(6)} %select_n.29), kind=kOutput, calls=%fused_computation.3 | convolution fusion | flops 1212152832 | bytes 6565892 | tf_op jit(solution)/shard_map/while/body/eval_jaxpr/cond/branch_1_fun/dot_general | solution.py:30
  192.7 8.2 %conditional.3 = ((f32[1024]{0:T(1024)S(1)}, f32[1024]{0:T(1024)S(1)}, f32[1024,512]{1,0:T(8,128)S(1)})) conditional(s32[]{:T(128)} %convert_element_type.82, (f32[1024]{0:T(1024)S(1)}, f32[1024]{0:T(1024)S(1)}, f32[1024,512]{1,0:T(8,128)S(1)}) %tuple.50, (s32[]{:T(128)}, s32[64]{0:T(128)S(1)}, bf16[576,8192]{1,0:T(8,128)(2,1)}, ...), branch_computations={%region_1.1_spmd, %region_2.4_spmd} | conditional | flops 2299530240 | bytes 20291918 | solution.py:93
  192.8 3.4 %fusion.2 = (f32[1024]{0:T(1024)S(1)}, f32[1024,1024]{1,0:T(8,128)S(1)}) fusion(s32[1024]{0:T(1024)S(1)} %le.27, s32[1024]{0:T(1024)S(1)} %iota_add_fusion, bf16[1024,576]{1,0:T(8,128)(2,1)S(1)} %get-tuple-element.214, bf16[576,8192]{1,0:T(8,128)(2,1)} %get-tuple-element.213, s32[]{:T(128)S(6)} %select_n.29), kind=kOutput, calls=%fused_computation.3 | convolution fusion | flops 1212152832 | bytes 6565892 | tf_op jit(solution)/shard_map/while/body/eval_jaxpr/cond/branch_1_fun/dot_general | solution.py:30
  197.9 3.0 %multiply_add_fusion = f32[1024,512]{1,0:T(8,128)S(1)} fusion(f32[1024,512]{1,0:T(8,128)S(1)} %get-tuple-element.216, f32[1024,1024]{1,0:T(8,128)S(1)} %get-tuple-element.275, f32[1024]{0:T(1024)S(1)} %max.4, s32[1024]{0:T(1024)S(1)} %le.27, s32[1024]{0:T(1024)S(1)} %iota_add_fusion, bf16[576,8192]{1,0:T(8,128)(2,1)} %get-tuple-element.213, ...), kind=kOutput, calls=%fused_computation.6 | convolution fusion | flops 1081081856 | bytes 9453572 | tf_op jit(solution)/shard_map/while/body/eval_jaxpr/cond/branch_1_fun/dot_general | solution.py:37
  200.9 8.2 %conditional.3 = ((f32[1024]{0:T(1024)S(1)}, f32[1024]{0:T(1024)S(1)}, f32[1024,512]{1,0:T(8,128)S(1)})) conditional(s32[]{:T(128)} %convert_element_type.82, (f32[1024]{0:T(1024)S(1)}, f32[1024]{0:T(1024)S(1)}, f32[1024,512]{1,0:T(8,128)S(1)}) %tuple.50, (s32[]{:T(128)}, s32[64]{0:T(128)S(1)}, bf16[576,8192]{1,0:T(8,128)(2,1)}, ...), branch_computations={%region_1.1_spmd, %region_2.4_spmd} | conditional | flops 2299530240 | bytes 20291918 | solution.py:93
  201.1 3.4 %fusion.2 = (f32[1024]{0:T(1024)S(1)}, f32[1024,1024]{1,0:T(8,128)S(1)}) fusion(s32[1024]{0:T(1024)S(1)} %le.27, s32[1024]{0:T(1024)S(1)} %iota_add_fusion, bf16[1024,576]{1,0:T(8,128)(2,1)S(1)} %get-tuple-element.214, bf16[576,8192]{1,0:T(8,128)(2,1)} %get-tuple-element.213, s32[]{:T(128)S(6)} %select_n.29), kind=kOutput, calls=%fused_computation.3 | convolution fusion | flops 1212152832 | bytes 6565892 | tf_op jit(solution)/shard_map/while/body/eval_jaxpr/cond/branch_1_fun/dot_general | solution.py:30
  215.3 13.2 %fusion.18 = bf16[7168,64]{0,1:T(8,128)(2,1)} fusion(bf16[2048,7168]{1,0:T(8,128)(2,1)} %param.15, bf16[16,8,8,128]{3,2,1,0:T(8,128)(2,1)S(1)} %fusion.22), kind=kOutput, calls=%fused_computation.21 | convolution fusion | flops 1879506944 | bytes 30539776 | tf_op jit(solution)/shard_map/dot_general | solution.py:107
  228.6 32.5 %reduce-scatter.2.cloned.1.call-done = bf16[1792,64]{0,1:T(8,128)(2,1)} async-done(((bf16[7168,64]{0,1:T(8,128)(2,1)}), bf16[1792,64]{0,1:T(8,128)(2,1)}) %reduce-scatter.2.cloned.1.call-update) | async-done | bytes 229392 | tf_op jit(solution)/shard_map/reduce_scatter | solution.py:106
  (117 shorter events, 64.9 us)
Async XLA Ops:
  6.5 105.1 %copy-start = (bf16[16,128,512]{2,1,0:T(8,128)(2,1)S(1)}, bf16[16,128,512]{2,1,0:T(8,128)(2,1)}, u32[]{:S(2)}) copy-start(bf16[16,128,512]{2,1,0:T(8,128)(2,1)} %param.13) | copy-start | bytes 6291460
  6.5 108.0 %copy-start.15 = (bf16[64,1024]{1,0:T(8,128)(2,1)S(1)}, bf16[64,1024]{1,0:T(8,128)(2,1)}, u32[]{:S(2)}) copy-start(bf16[64,1024]{1,0:T(8,128)(2,1)} %param.12) | copy-start | bytes 393220
  6.5 254.5 %reduce-scatter.2.cloned.1.call-start = ((), (), s32[]{:S(2)}) async-start(), calls=%async_computation.1 | async-start | bytes 1146880 | tf_op jit(solution)/shard_map/reduce_scatter | solution.py:106
  6.5 17.5 %collective-permute-start = (bf16[576,1024]{1,0:T(8,128)(2,1)}, bf16[576,1024]{1,0:T(8,128)(2,1)S(1)}, u32[]{:S(2)}, u32[]{:S(2)}) collective-permute-start(bf16[576,1024]{1,0:T(8,128)(2,1)} %param.16), channel_id=1, source_target_pairs={{0,4},{4,8},{8,12},{12,16},{16,20},{20,24},{24,28},{28,0},{1,5},{5... | collective-permute-start | bytes 3538952 | tf_op jit(solution)/shard_map/ppermute | solution.py:83
  24.0 16.5 %collective-permute-start.1 = (bf16[576,1024]{1,0:T(8,128)(2,1)S(1)}, bf16[576,1024]{1,0:T(8,128)(2,1)S(1)}, u32[]{:S(2)}, u32[]{:S(2)}) collective-permute-start(bf16[576,1024]{1,0:T(8,128)(2,1)S(1)} %collective-permute-done), channel_id=1, source_target_pairs={{0,4},{4,8},{8,12},{12,16},{16,20},{20,24},{24,28},{28,0},{1,5},{5... | collective-permute-start | bytes 3538952 | tf_op jit(solution)/shard_map/ppermute | solution.py:83
  40.5 1.0 copy-start.5
  41.6 16.5 %collective-permute-start.2 = (bf16[576,1024]{1,0:T(8,128)(2,1)S(1)}, bf16[576,1024]{1,0:T(8,128)(2,1)S(1)}, u32[]{:S(2)}, u32[]{:S(2)}) collective-permute-start(bf16[576,1024]{1,0:T(8,128)(2,1)S(1)} %collective-permute-done.1), channel_id=1, source_target_pairs={{0,4},{4,8},{8,12},{12,16},{16,20},{20,24},{24,28},{28,0},{1,5},{5... | collective-permute-start | bytes 3538952 | tf_op jit(solution)/shard_map/ppermute | solution.py:83
  58.1 1.0 copy-start.7
  59.1 16.5 %collective-permute-start.3 = (bf16[576,1024]{1,0:T(8,128)(2,1)S(1)}, bf16[576,1024]{1,0:T(8,128)(2,1)S(1)}, u32[]{:S(2)}, u32[]{:S(2)}) collective-permute-start(bf16[576,1024]{1,0:T(8,128)(2,1)S(1)} %collective-permute-done.2), channel_id=1, source_target_pairs={{0,4},{4,8},{8,12},{12,16},{16,20},{20,24},{24,28},{28,0},{1,5},{5... | collective-permute-start | bytes 3538952 | tf_op jit(solution)/shard_map/ppermute | solution.py:83
  75.7 1.1 copy-start.9
  76.8 16.5 %collective-permute-start.4 = (bf16[576,1024]{1,0:T(8,128)(2,1)S(1)}, bf16[576,1024]{1,0:T(8,128)(2,1)S(1)}, u32[]{:S(2)}, u32[]{:S(2)}) collective-permute-start(bf16[576,1024]{1,0:T(8,128)(2,1)S(1)} %collective-permute-done.3), channel_id=1, source_target_pairs={{0,4},{4,8},{8,12},{12,16},{16,20},{20,24},{24,28},{28,0},{1,5},{5... | collective-permute-start | bytes 3538952 | tf_op jit(solution)/shard_map/ppermute | solution.py:83
  93.3 1.0 copy-start.11
  94.3 16.6 %collective-permute-start.5 = (bf16[576,1024]{1,0:T(8,128)(2,1)S(1)}, bf16[576,1024]{1,0:T(8,128)(2,1)}, u32[]{:S(2)}, u32[]{:S(2)}) collective-permute-start(bf16[576,1024]{1,0:T(8,128)(2,1)S(1)} %collective-permute-done.4), channel_id=1, source_target_pairs={{0,4},{4,8},{8,12},{12,16},{16,20},{20,24},{24,28},{28,0},{1,5},{5... | collective-permute-start | bytes 3538952 | tf_op jit(solution)/shard_map/ppermute | solution.py:83
  111.0 16.8 %collective-permute-start.6 = (bf16[576,1024]{1,0:T(8,128)(2,1)}, bf16[576,1024]{1,0:T(8,128)(2,1)}, u32[]{:S(2)}, u32[]{:S(2)}) collective-permute-start(bf16[576,1024]{1,0:T(8,128)(2,1)} %collective-permute-done.5), channel_id=1, source_target_pairs={{0,4},{4,8},{8,12},{12,16},{16,20},{20,24},{24,28},{28,0},{1,5},{5... | collective-permute-start | bytes 3538952 | tf_op jit(solution)/shard_map/ppermute | solution.py:83
  114.6 18.1 %copy-start.12 = (bf16[576,1024]{1,0:T(8,128)(2,1)S(1)}, bf16[576,1024]{1,0:T(8,128)(2,1)}, u32[]{:S(2)}) copy-start(bf16[576,1024]{1,0:T(8,128)(2,1)} %copy-done.11) | copy-start | bytes 3538948
  114.8 18.9 %copy-start.10 = (bf16[576,1024]{1,0:T(8,128)(2,1)S(1)}, bf16[576,1024]{1,0:T(8,128)(2,1)}, u32[]{:S(2)}) copy-start(bf16[576,1024]{1,0:T(8,128)(2,1)} %copy-done.9) | copy-start | bytes 3538948
  117.3 17.5 %copy-start.8 = (bf16[576,1024]{1,0:T(8,128)(2,1)S(1)}, bf16[576,1024]{1,0:T(8,128)(2,1)}, u32[]{:S(2)}) copy-start(bf16[576,1024]{1,0:T(8,128)(2,1)} %copy-done.7) | copy-start | bytes 3538948
  130.2 5.7 %copy-start.6 = (bf16[576,1024]{1,0:T(8,128)(2,1)S(1)}, bf16[576,1024]{1,0:T(8,128)(2,1)}, u32[]{:S(2)}) copy-start(bf16[576,1024]{1,0:T(8,128)(2,1)} %copy-done.5) | copy-start | bytes 3538948
  133.7 4.4 %copy-start.4 = (bf16[576,1024]{1,0:T(8,128)(2,1)S(1)}, bf16[576,1024]{1,0:T(8,128)(2,1)}, u32[]{:S(2)}) copy-start(bf16[576,1024]{1,0:T(8,128)(2,1)} %param.16) | copy-start | bytes 3538948
  137.0 7.0 %copy-start.13 = (bf16[576,1024]{1,0:T(8,128)(2,1)S(1)}, bf16[576,1024]{1,0:T(8,128)(2,1)}, u32[]{:S(2)}) copy-start(bf16[576,1024]{1,0:T(8,128)(2,1)} %copy-done.11) | copy-start | bytes 3538948
  150.6 8.9 %copy-start.14 = (bf16[1024,576]{1,0:T(8,128)(2,1)S(1)}, bf16[1024,576]{1,0:T(8,128)(2,1)}, u32[]{:S(2)}) copy-start(bf16[1024,576]{1,0:T(8,128)(2,1)} %pad_maximum_fusion) | copy-start | bytes 3538948
  209.2 1.3 copy-start.2
  209.2 3.2 %copy-start.3 = (bf16[16,512,128]{2,1,0:T(8,128)(2,1)S(1)}, bf16[16,512,128]{2,1,0:T(8,128)(2,1)}, u32[]{:S(2)}) copy-start(bf16[16,512,128]{2,1,0:T(8,128)(2,1)} %param.14) | copy-start | bytes 6291460
  215.3 45.7 %copy-start.1 = (bf16[16,128,512]{2,1,0:T(8,128)(2,1)S(1)}, bf16[16,128,512]{2,1,0:T(8,128)(2,1)}, u32[]{:S(2)}) copy-start(bf16[16,128,512]{2,1,0:T(8,128)(2,1)} %param.13) | copy-start | bytes 6291460
Sparse Core Ops, SparseCore 0:
  228.7 32.2 reduce-scatter.1
